TPU v7x, 32 devices: a whole 2x2x4 slice. The times are simulated.
32 devices in a mesh: front: 8 (over z, core), tile: 4 (over y, x).
Axes of the slice: x: 2, y: 2, z: 4, core: 2. Of those that a mesh axis runs over, the one named last changes fastest.
Arguments:
- child_rhs: float32 [8, 2048, 256], P('front', 'tile'), may hold values from -6 to 6
- child_lower: float32 [8, 2048, 2048], P('front', 'tile'), as said below
- child_border: float32 [8, 2048, 2048], P('front', 'tile'), may hold values from -0.125 to 0.125
- child_upper_border: float32 [8, 2048, 2048], P('front', 'tile'), may hold values from -0.125 to 0.125
- child_upper: float32 [8, 2048, 2048], P('front', 'tile'), as said below
- parent_rhs: float32 [8, 512, 256], P('front', 'tile'), may hold values from -6 to 6
- parent_lower: float32 [8, 512, 2048], P('front', 'tile'), as said below
- parent_upper: float32 [8, 512, 2048], P('front', 'tile'), as said below
- border_map: int32 [8, 2048], P('front'), may hold values from 0 to 2047, as said below
- border_count: int32 [8], P('front'), may hold values from 512 to 2048, as said below
Outputs:
- child_solution: float32 [8, 2048, 256], P('front', 'tile')
- parent_solution: float32 [8, 512, 256], P('front', 'tile')
Inputs may be any that keep to these rules, and one draw needn't show every extreme that they name: `border_map`: within one child the 2048 entries are distinct parent rows. Group g of parent rows holds the rows m with (m mod (512)) // 128 = g, for g below 4. In every aligned block of 512 border rows of a child, each group receives either no row or exactly 256 rows, and each group receives 2048 // 4 border rows of the child in all. `border_count`: some child has all 2048 border rows live. `child_lower`: lower triangular including the diagonal. `child_upper`: upper triangular including the diagonal. `parent_lower`: each parent's 2048 rows form a lower triangular matrix including the diagonal. `parent_upper`: each parent's 2048 rows form an upper triangular matrix including the diagonal.
All inputs are finite; a program needn't handle non-finite values.
Results may differ from a plain program's by a relative error of at most 0.00013.
Values sent between devices are 32-bit elements; how exact they have to be, the bound alone decides.
A program may use at most 64 MiB of HBM per device.

v0:
```python
import jax
import jax.numpy as jnp
from jax import lax
from jax.sharding import PartitionSpec as P


def partner_2(block, axis, apart):
    count = lax.axis_size(axis)
    route = []
    for low in range(count):
        high = low | 1 << apart
        if high != low and high < count:
            route += [(low, high), (high, low)]
    return lax.ppermute(block, axis, route)


def product(matrix, vector):
    return jnp.dot(
        matrix, vector, preferred_element_type=jnp.float32, precision=lax.Precision.HIGHEST
    )


def apply_rows(matrix, local_rows):
    return product(matrix, lax.all_gather(local_rows, "tile", axis=0, tiled=True))


def pair_quarters(stacked, quarter):
    for bit_number in (0, 1):
        partner = partner_2(stacked, "front", bit_number)
        upper_bit = jnp.right_shift(quarter, bit_number) % 2
        stacked = jnp.where(
            upper_bit == 0,
            jnp.concatenate([stacked, partner], 0),
            jnp.concatenate([partner, stacked], 0),
        )
    return stacked


def assemble(block, quarter):
    whole_quarter = lax.all_gather(block, "tile", axis=0, tiled=True)
    stacked = pair_quarters(whole_quarter[None], quarter)
    return stacked.reshape(-1, block.shape[1])


def layout_index(parent_row, quarter_rows, slab_rows):
    return (
        parent_row % quarter_rows // slab_rows * (4 * slab_rows)
        + parent_row // quarter_rows * slab_rows
        + parent_row % slab_rows
    )


def local(
    child_rhs,
    child_lower,
    child_border,
    child_upper_border,
    child_upper,
    parent_rhs,
    parent_lower,
    parent_upper,
    border_map,
    border_count,
):
    tile_pos = lax.axis_index("tile")
    quarter = lax.axis_index("front") % 4
    border_rows = child_border.shape[1]
    slab_rows = parent_lower.shape[1]
    parent_rows = parent_lower.shape[2]
    quarter_rows = parent_rows // 4
    slab_width = 4 * slab_rows
    live_total = border_count[0]
    map_whole = border_map[0]
    forward_child = apply_rows(child_lower[0], child_rhs[0])
    own_ids = tile_pos * border_rows + jnp.arange(border_rows, dtype=jnp.int32)
    own_map = lax.dynamic_slice_in_dim(map_whole, tile_pos * border_rows, border_rows, 0)
    alive_rows = own_ids < live_total
    update = -apply_rows(child_border[0], forward_child)
    update = jnp.where(alive_rows[:, None], update, 0.0)
    target = layout_index(own_map, quarter_rows, slab_rows)
    target = jnp.where(alive_rows, target, -1)
    row_ids = jnp.arange(slab_width * lax.axis_size("tile"), dtype=jnp.int32)
    selector = (row_ids[:, None] == target[None, :]).astype(jnp.float32)
    scattered = lax.psum_scatter(product(selector, update), "tile", scatter_dimension=0, tiled=True)
    stacked = scattered.reshape(4, slab_rows, scattered.shape[1])
    for bit_number in (1, 0):
        half_size = stacked.shape[0] // 2
        upper_bit = jnp.right_shift(quarter, bit_number) % 2
        retained = lax.dynamic_slice_in_dim(stacked, upper_bit * half_size, half_size, 0)
        sending = lax.dynamic_slice_in_dim(stacked, (1 - upper_bit) * half_size, half_size, 0)
        stacked = retained + partner_2(sending, "front", bit_number)
    gathered = stacked[0]
    right_parent = parent_rhs[0] + gathered
    forward_parent = product(parent_lower[0], assemble(right_parent, quarter))
    solved_parent = product(parent_upper[0], assemble(forward_parent, quarter))
    parent_whole = assemble(solved_parent, quarter)
    selector = (
        (own_map[:, None] == jnp.arange(parent_rows, dtype=jnp.int32)[None, :])
        & alive_rows[:, None]
    ).astype(jnp.float32)
    border_values = product(selector, parent_whole)
    reduced = forward_child - apply_rows(child_upper_border[0], border_values)
    child_solution = apply_rows(child_upper[0], reduced)
    return (child_solution[None], solved_parent[None])


def solution(mesh):
    return jax.shard_map(
        local,
        mesh=mesh,
        in_specs=(
            P("front", "tile", None),
            P("front", "tile", None),
            P("front", "tile", None),
            P("front", "tile", None),
            P("front", "tile", None),
            P("front", "tile", None),
            P("front", "tile", None),
            P("front", "tile", None),
            P("front", None),
            P("front"),
        ),
        out_specs=(P("front", "tile", None), P("front", "tile", None)),
        check_vma=False,
    )
```

profile of v0, /device:TPU:0, one launch (start us, length us, event | category | flops | bytes accessed | tf_op | source)
XLA Modules:
  0.0 388.4 jit_solution(4923493146791884085)
XLA Ops:
  7.2 0.7 all-gather.13.cloned.1.call-update
  8.0 39.9 %all-gather.13.cloned.1.call-done = f32[1,2048,256]{2,1,0:T(8,128)} async-done(((f32[1,512,256]{2,1,0:T(8,128)}), f32[1,2048,256]{2,1,0:T(8,128)}) %all-gather.13.cloned.1.call-update) | async-done | bytes 2097168 | tf_op jit(solution)/shard_map/all_gather | solution.py:24
  47.9 7.1 %fusion.6 = f32[512,256]{1,0:T(8,128)} fusion(f32[1,512,2048]{2,1,0:T(8,128)} %param.11, f32[1,2048,256]{2,1,0:T(8,128)} %all-gather.13.cloned.1.call-done), kind=kOutput, calls=%fused_computation.6 | convolution fusion | flops 3221225472 | bytes 6815744 | tf_op jit(solution)/shard_map/dot_general | solution.py:18
  55.0 0.0 reduce-scatter.2.cloned.1.call-start
  55.7 0.7 compare_select_fusion
  56.5 34.0 %all-gather.7.cloned.1.call-done = f32[2048,256]{1,0:T(8,128)} async-done(((f32[512,256]{1,0:T(8,128)}), f32[2048,256]{1,0:T(8,128)}) %all-gather.7.cloned.1.call-update) | async-done | bytes 2097168 | tf_op jit(solution)/shard_map/all_gather | solution.py:24
  90.5 9.3 %fusion.19 = f32[256,512]{1,0:T(8,128)S(1)} fusion(f32[2048,256]{1,0:T(8,128)} %all-gather.7.cloned.1.call-done, f32[1,512,2048]{2,1,0:T(8,128)} %param.12, pred[512]{0:T(512)(128)(4,1)S(1)} %add_compare_fusion), kind=kOutput, calls=%fused_computation.21 | convolution fusion | flops 3221487616 | bytes 6816256 | tf_op jit(solution)/shard_map/dot_general | solution.py:18
  99.8 3.3 fusion.11
  103.2 35.3 %reduce-scatter.2.cloned.1.call-done = f32[512,256]{1,0:T(8,128)} async-done(((f32[2048,256]{1,0:T(8,128)}), f32[512,256]{1,0:T(8,128)}) %reduce-scatter.2.cloned.1.call-update) | async-done | bytes 524304 | tf_op jit(solution)/shard_map/reduce_scatter | solution.py:84
  138.5 1.1 constant_dynamic-slice_fusion.1
  139.6 0.1 copy.26
  139.7 1.6 collective-permute-start
  141.2 0.1 copy.25
  141.4 6.4 %collective-permute-done = f32[2,128,256]{1,2,0:T(8,128)S(1)} collective-permute-done((f32[2,128,256]{1,2,0:T(8,128)S(1)}, f32[2,128,256]{1,2,0:T(8,128)S(1)}, u32[]{:S(2)}, u32[]{:S(2)}) %collective-permute-start) | collective-permute-done | bytes 262176 | tf_op jit(solution)/shard_map/ppermute | solution.py:14
  147.9 0.1 collective-permute-start.1
  148.0 0.1 copy.19
  148.1 1.2 collective-permute-done.1
  149.3 14.2 %all-gather.1 = f32[1,512,256]{1,2,0:T(8,128)S(1)} all-gather(f32[1,128,256]{1,2,0:T(8,128)S(1)} %add_add_fusion), channel_id=3, replica_groups=mesh['front'=8,'tile'=4] {'tile'}, dimensions={1}, use_global_device_ids=true | all-gather | bytes 655360 | tf_op jit(solution)/shard_map/all_gather | solution.py:40
  163.5 1.9 collective-permute-done.2
  165.5 0.1 maximum_select_fusion.3
  165.6 1.6 collective-permute-start.3
  167.1 23.8 %collective-permute-done.3 = f32[2,512,256]{1,2,0:T(8,128)} collective-permute-done((f32[2,512,256]{1,2,0:T(8,128)S(1)}, f32[2,512,256]{1,2,0:T(8,128)}, u32[]{:S(2)}, u32[]{:S(2)}) %collective-permute-start.3) | collective-permute-done | bytes 1048608 | tf_op jit(solution)/shard_map/ppermute | solution.py:14
  191.0 2.7 maximum_select_fusion
  193.6 1.8 copy.20
  195.5 5.0 %convolution_bitcast_fusion = f32[128,256]{0,1:T(8,128)S(1)} fusion(f32[2048,256]{1,0:T(8,128)} %bitcast.62, f32[1,128,2048]{2,1,0:T(8,128)S(1)} %copy-done), kind=kOutput, calls=%fused_computation.25 | convolution fusion | flops 805306368 | bytes 3276800 | tf_op jit(solution)/shard_map/dot_general | solution.py:18
  200.5 11.5 %all_gather.24 = f32[512,256]{0,1:T(8,128)S(1)} all-gather(f32[128,256]{0,1:T(8,128)S(1)} %convolution_bitcast_fusion), channel_id=1, replica_groups=mesh['front'=8,'tile'=4] {'tile'}, dimensions={0}, use_global_device_ids=true | all-gather | bytes 655360 | tf_op jit(solution)/shard_map/all_gather | solution.py:40
  212.0 1.9 collective-permute-done.4
  213.9 0.1 maximum_select_fusion.4
  214.1 1.6 collective-permute-start.5
  215.6 23.7 %collective-permute-done.5 = f32[2,512,256]{1,2,0:T(8,128)S(1)} collective-permute-done((f32[2,512,256]{1,2,0:T(8,128)S(1)}, f32[2,512,256]{1,2,0:T(8,128)S(1)}, u32[]{:S(2)}, u32[]{:S(2)}) %collective-permute-start.5) | collective-permute-done | bytes 1048608 | tf_op jit(solution)/shard_map/ppermute | solution.py:14
  239.3 0.2 maximum_select_fusion.1
  239.6 1.8 copy.21
  241.4 5.3 %fusion.31 = f32[256,128]{1,0:T(8,128)S(1)} fusion(f32[2048,256]{1,0:T(8,128)} %bitcast.63, f32[1,128,2048]{2,1,0:T(8,128)} %param.17), kind=kOutput, calls=%fused_computation.29 | convolution fusion | flops 805306368 | bytes 3276800 | tf_op jit(solution)/shard_map/dot_general | solution.py:18
  246.7 12.5 %all_gather.25 = f32[512,256]{0,1:T(8,128)S(1)} all-gather(f32[128,256]{0,1:T(8,128)S(1)} %bitcast.69), channel_id=1, replica_groups=mesh['front'=8,'tile'=4] {'tile'}, dimensions={0}, use_global_device_ids=true | all-gather | bytes 655360 | tf_op jit(solution)/shard_map/all_gather | solution.py:40
  259.2 1.9 collective-permute-done.6
  261.1 0.1 maximum_select_fusion.5
  261.2 1.6 collective-permute-start.7
  262.8 23.7 %collective-permute-done.7 = f32[2,512,256]{1,2,0:T(8,128)S(1)} collective-permute-done((f32[2,512,256]{1,2,0:T(8,128)S(1)}, f32[2,512,256]{1,2,0:T(8,128)S(1)}, u32[]{:S(2)}, u32[]{:S(2)}) %collective-permute-start.7) | collective-permute-done | bytes 1048608 | tf_op jit(solution)/shard_map/ppermute | solution.py:14
  286.5 0.2 maximum_select_fusion.2
  286.8 1.8 copy.22
  288.6 4.9 %fusion.9 = f32[512,256]{1,0:T(8,128)} fusion(f32[2048,256]{1,0:T(8,128)} %bitcast.68, s32[512]{0:T(512)S(1)} %bitcast.72, pred[512]{0:T(512)(128)(4,1)S(1)} %add_compare_fusion), kind=kOutput, calls=%fused_computation.11 | convolution fusion | flops 3223322624 | bytes 2624000 | tf_op jit(solution)/shard_map/dot_general | solution.py:18
  293.5 0.0 all-gather.11.cloned.1.call-start
  293.5 35.4 %all-gather.9.cloned.1.call-done = f32[2048,256]{1,0:T(8,128)} async-done(((f32[512,256]{1,0:T(8,128)}), f32[2048,256]{1,0:T(8,128)}) %all-gather.9.cloned.1.call-update) | async-done | bytes 2097168 | tf_op jit(solution)/shard_map/all_gather | solution.py:24
  329.0 7.1 %fusion.28 = f32[512,256]{1,0:T(8,128)} fusion(f32[512,256]{1,0:T(8,128)S(1)} %copy-done.1, f32[2048,256]{1,0:T(8,128)} %all-gather.9.cloned.1.call-done, f32[1,512,2048]{2,1,0:T(8,128)} %param.13), kind=kOutput, calls=%fused_computation.24 | convolution fusion | flops 3221356544 | bytes 7340032 | tf_op jit(solution)/shard_map/dot_general | solution.py:18
  336.1 0.8 copy.24
  336.9 34.7 %all-gather.11.cloned.1.call-done = f32[2048,256]{1,0:T(8,128)} async-done(((f32[512,256]{1,0:T(8,128)}), f32[2048,256]{1,0:T(8,128)}) %all-gather.11.cloned.1.call-update) | async-done | bytes 2097168 | tf_op jit(solution)/shard_map/all_gather | solution.py:24
  371.6 9.3 %fusion.25 = f32[1,512,256]{1,2,0:T(8,128)S(1)} fusion(f32[2048,256]{1,0:T(8,128)} %all-gather.11.cloned.1.call-done, f32[1,512,2048]{2,1,0:T(8,128)} %param.14), kind=kOutput, calls=%fused_computation.23 | convolution fusion | flops 3221225472 | bytes 6815744 | tf_op jit(solution)/shard_map/dot_general | solution.py:18
  380.9 1.0 copy.23
  (22 shorter events, 0.3 us)
Async XLA Ops:
  7.2 188.3 %copy-start = (f32[1,128,2048]{2,1,0:T(8,128)S(1)}, f32[1,128,2048]{2,1,0:T(8,128)}, u32[]{:S(2)}) copy-start(f32[1,128,2048]{2,1,0:T(8,128)} %param.16) | copy-start | bytes 3145732
  7.2 40.7 %all-gather.13.cloned.1.call-start = ((), (), s32[]{:S(2)}) async-start(), calls=%async_computation.5 | async-start | bytes 2621440 | tf_op jit(solution)/shard_map/all_gather | solution.py:24
  7.9 82.6 %all-gather.7.cloned.1.call-start = ((), (), s32[]{:S(2)}) async-start(), calls=%async_computation.1 | async-start | bytes 2621440 | tf_op jit(solution)/shard_map/all_gather | solution.py:24
  55.0 83.5 %reduce-scatter.2.cloned.1.call-start = ((), (), s32[]{:S(2)}) async-start(), calls=%async_computation.2 | async-start | bytes 2621440 | tf_op jit(solution)/shard_map/reduce_scatter | solution.py:84
  103.1 44.8 %copy-start.3 = (f32[1,128,256]{2,1,0:T(8,128)S(1)}, f32[1,128,256]{2,1,0:T(8,128)}, u32[]{:S(2)}) copy-start(f32[1,128,256]{2,1,0:T(8,128)} %param.15) | copy-start | bytes 393220
  103.1 225.8 %all-gather.9.cloned.1.call-start = ((), (), s32[]{:S(2)}) async-start(), calls=%async_computation.3 | async-start | bytes 2621440 | tf_op jit(solution)/shard_map/all_gather | solution.py:24
  139.7 8.1 %collective-permute-start = (f32[2,128,256]{1,2,0:T(8,128)S(1)}, f32[2,128,256]{1,2,0:T(8,128)S(1)}, u32[]{:S(2)}, u32[]{:S(2)}) collective-permute-start(f32[2,128,256]{1,2,0:T(8,128)S(1)} %copy.26), channel_id=1, source_target_pairs={{0,8},{8,0},{4,12},{12,4},{16,24},{24,16},{20,28},{28,20},{1,9},{9... | collective-permute-start | bytes 786440 | tf_op jit(solution)/shard_map/ppermute | solution.py:14
  147.9 1.4 collective-permute-start.1
  163.5 1.9 collective-permute-start.2
  165.6 1.6 copy-start.2
  165.6 25.4 %collective-permute-start.3 = (f32[2,512,256]{1,2,0:T(8,128)S(1)}, f32[2,512,256]{1,2,0:T(8,128)}, u32[]{:S(2)}, u32[]{:S(2)}) collective-permute-start(f32[2,512,256]{1,2,0:T(8,128)S(1)} %maximum_select_fusion.3), channel_id=1, source_target_pairs={{0,8},{8,0},{4,12},{12,4},{16,24},{24,16},{20,28},{28,20},{1,9},{9... | collective-permute-start | bytes 3145736 | tf_op jit(solution)/shard_map/ppermute | solution.py:14
  212.0 1.9 collective-permute-start.4
  214.1 25.3 %collective-permute-start.5 = (f32[2,512,256]{1,2,0:T(8,128)S(1)}, f32[2,512,256]{1,2,0:T(8,128)S(1)}, u32[]{:S(2)}, u32[]{:S(2)}) collective-permute-start(f32[2,512,256]{1,2,0:T(8,128)S(1)} %maximum_select_fusion.4), channel_id=1, source_target_pairs={{0,8},{8,0},{4,12},{12,4},{16,24},{24,16},{20,28},{28,20},{1,9},{9... | collective-permute-start | bytes 3145736 | tf_op jit(solution)/shard_map/ppermute | solution.py:14
  259.2 1.9 collective-permute-start.6
  261.2 25.3 %collective-permute-start.7 = (f32[2,512,256]{1,2,0:T(8,128)S(1)}, f32[2,512,256]{1,2,0:T(8,128)S(1)}, u32[]{:S(2)}, u32[]{:S(2)}) collective-permute-start(f32[2,512,256]{1,2,0:T(8,128)S(1)} %maximum_select_fusion.5), channel_id=1, source_target_pairs={{0,8},{8,0},{4,12},{12,4},{16,24},{24,16},{20,28},{28,20},{1,9},{9... | collective-permute-start | bytes 3145736 | tf_op jit(solution)/shard_map/ppermute | solution.py:14
  288.6 40.4 %copy-start.1 = (f32[512,256]{1,0:T(8,128)S(1)}, f32[512,256]{1,0:T(8,128)}, u32[]{:S(2)}) copy-start(f32[512,256]{1,0:T(8,128)} %fusion.6) | copy-start | bytes 1572868
  293.5 78.1 %all-gather.11.cloned.1.call-start = ((), (), s32[]{:S(2)}) async-start(), calls=%async_computation.4 | async-start | bytes 2621440 | tf_op jit(solution)/shard_map/all_gather | solution.py:24
Sparse Core Ops, SparseCore 0:
  9.9 38.0 all-gather.12
  55.1 35.3 all-gather.6
  103.3 35.1 reduce-scatter.1
  293.6 35.3 all-gather.8
  336.2 35.3 all-gather.10
where the time goes:
time: 389 us; the launch traced here: 388 us
  waiting for transfers between devices  265 us (68%)
  matrix products  51.3 us (13%)
  blocking collectives  38.3 us (10%)
  between operations  14.7 us (4%)
  local copies, waits for them, and re-layouts  8.67 us (2%)
  starting transfers between devices  6.48 us (2%)
  other arithmetic  4.29 us (1%)
    all_gather x4, waiting for transfers between devices, apply_rows(): lax.all_gather(local_rows, 'tile', axis=0, tiled=True)  144 us
    ppermute x8, waiting for transfers between devices, partner_2(): return lax.ppermute(block, axis, route)  84.6 us
    dot_general x8, matrix products, product(): jnp.dot(matrix, vector, preferred_element_type=jnp.float32, precision=lax...  51.3 us
    all_gather x3, blocking collectives, assemble(): whole_quarter = lax.all_gather(block, 'tile', axis=0, tiled=True)  38.3 us
    reduce_scatter x1, waiting for transfers between devices, local(): lax.psum_scatter(product(selector, update), 'tile', scatter_dimension=0,...  35.3 us
  transfers between devices with their start and end apart: 13, of which 13 were waited for; matrix products, arithmetic and copies ran while one was open for 0% of the time, Pallas kernels for 0%

commit v1 on v0

--- a/solution.py
+++ b/solution.py
@@ -2,6 +2,27 @@
 import jax.numpy as jnp
 from jax import lax
 from jax.sharding import PartitionSpec as P
+
+
+def ring_gather(x, axis, dim):
+    size, index, rows = (lax.axis_size(axis), lax.axis_index(axis), x.shape[dim])
+    right = [(i, (i + 1) % size) for i in range(size)]
+    backward = [(i, (i - 1) % size) for i in range(size)]
+    whole = jnp.zeros((*x.shape[:dim], size * rows, *x.shape[dim + 1 :]), x.dtype)
+    whole = lax.dynamic_update_slice_in_dim(whole, x, index * rows, axis=dim)
+    from_left = from_right = x
+    middle = size // 2
+    for hop in range(1, middle + 1):
+        from_left = lax.ppermute(from_left, axis, right)
+        whole = lax.dynamic_update_slice_in_dim(
+            whole, from_left, (index - hop) % size * rows, axis=dim
+        )
+        if hop < size - middle:
+            from_right = lax.ppermute(from_right, axis, backward)
+            whole = lax.dynamic_update_slice_in_dim(
+                whole, from_right, (index + hop) % size * rows, axis=dim
+            )
+    return whole
 
 
 def partner_2(block, axis, apart):
@@ -21,7 +42,7 @@
 
 
 def apply_rows(matrix, local_rows):
-    return product(matrix, lax.all_gather(local_rows, "tile", axis=0, tiled=True))
+    return product(matrix, ring_gather(local_rows, "tile", 0))
 
 
 def pair_quarters(stacked, quarter):

time: 389 us -> 385 us (0.990)
  waiting for transfers between devices: 265 us -> 236 us
  local copies, waits for them, and re-layouts: 8.67 us -> 30.9 us
  starting transfers between devices: 6.48 us -> 20.4 us
  matrix products: 51.3 us -> 39.3 us
    all_gather x4 -> x0, waiting for transfers between devices: 144 us -> none  [apply_rows(): lax.all_gather(local_rows, 'tile', axis=0, tiled=True)]
    ppermute x0 -> x12, waiting for transfers between devices: none -> 116 us  [the longest x8 83.1 us: ring_gather(): from_left = lax.ppermute(from_left, axis, right)]
    ppermute x0 -> x12, starting transfers between devices: none -> 14 us  [the longest x4 8.39 us: ring_gather(): from_right = lax.ppermute(from_right, axis, backward)]
    dot_general x8, matrix products: 51.3 us -> 39.3 us  [product(): jnp.dot(matrix, vector, preferred_element_type=jnp.float32, precision=lax...]
    dynamic_update_slice x0 -> x14, local copies, waits for them, and re-layouts: none -> 9.08 us  [the longest x8 5.09 us: ring_gather(): lax.dynamic_update_slice_in_dim(whole, from_left, (index - hop) % size *...]
    ppermute x0 -> x6, local copies, waits for them, and re-layouts: none -> 6.69 us  [the longest x4 4.46 us: ring_gather(): from_left = lax.ppermute(from_left, axis, right)]
  transfers between devices with their start and end apart: 13 -> 21, of which waited for: 13 -> 21; matrix products, arithmetic and copies ran while one was open for 0% -> 4% of each run, Pallas kernels for 0% -> 0%
where the time goes in v1:
time: 385 us; the launch traced here: 384 us
  waiting for transfers between devices  236 us (61%)
  matrix products  39.3 us (10%)
  blocking collectives  38.3 us (10%)
  local copies, waits for them, and re-layouts  30.9 us (8%)
  starting transfers between devices  20.4 us (5%)
  between operations  15.1 us (4%)
  other arithmetic  4.42 us (1%)
    ppermute x8, waiting for transfers between devices, partner_2(): return lax.ppermute(block, axis, route)  84.6 us
    ppermute x8, waiting for transfers between devices, ring_gather(): from_left = lax.ppermute(from_left, axis, right)  83.1 us
    dot_general x8, matrix products, product(): jnp.dot(matrix, vector, preferred_element_type=jnp.float32, precision=lax...  39.3 us
    all_gather x3, blocking collectives, assemble(): whole_quarter = lax.all_gather(block, 'tile', axis=0, tiled=True)  38.3 us
    reduce_scatter x1, waiting for transfers between devices, local(): lax.psum_scatter(product(selector, update), 'tile', scatter_dimension=0,...  35.5 us
    ppermute x4, waiting for transfers between devices, ring_gather(): from_right = lax.ppermute(from_right, axis, backward)  32.8 us
    ppermute x4, starting transfers between devices, ring_gather(): from_right = lax.ppermute(from_right, axis, backward)  8.39 us
  transfers between devices with their start and end apart: 21, of which 21 were waited for; matrix products, arithmetic and copies ran while one was open for 4% of the time, Pallas kernels for 0%

profile of v1, /device:TPU:0, one launch (start us, length us, event | category | flops | bytes accessed | tf_op | source)
XLA Modules:
  0.0 384.4 jit_solution(5707614444389954158)
XLA Ops:
  7.2 3.0 collective-permute-start
  11.2 13.0 %collective-permute-done = f32[512,256]{1,0:T(8,128)} collective-permute-done((f32[512,256]{1,0:T(8,128)}, f32[512,256]{1,0:T(8,128)}, u32[]{:S(2)}, u32[]{:S(2)}) %collective-permute-start) | collective-permute-done | bytes 524320 | tf_op jit(solution)/shard_map/ppermute | solution.py:16
  25.3 2.0 copy.25
  28.5 2.0 copy.26
  30.5 5.5 %collective-permute-done.1 = f32[512,256]{1,0:T(8,128)} collective-permute-done((f32[512,256]{1,0:T(8,128)}, f32[512,256]{1,0:T(8,128)}, u32[]{:S(2)}, u32[]{:S(2)}) %collective-permute-start.1) | collective-permute-done | bytes 524320 | tf_op jit(solution)/shard_map/ppermute | solution.py:21
  36.0 2.0 copy.27
  40.3 5.6 %collective-permute-done.2 = f32[512,256]{1,0:T(8,128)} collective-permute-done((f32[512,256]{1,0:T(8,128)}, f32[512,256]{1,0:T(8,128)}, u32[]{:S(2)}, u32[]{:S(2)}) %collective-permute-start.2) | collective-permute-done | bytes 524320 | tf_op jit(solution)/shard_map/ppermute | solution.py:16
  45.9 2.0 copy.28
  49.3 5.5 %constant_dynamic-update-slice_fusion.11 = (f32[2048,256]{0,1:T(8,128)S(1)}, f32[512,256]{0,1:T(8,128)S(1)}) fusion(f32[2048,256]{0,1:T(8,128)S(1)} %broadcast.99.clone, s32[]{:T(128)S(6)} %select_n.182, f32[2048,256]{0,1:T(8,128)S(1)} %constant_dynamic-update-slice_fusion.12, f32[1,512,2048]{2,1,0:T(8,128)} %param.11), kind=kOutput, calls=%fused_computation.52 | convolution fusion | flops 3221225472 | bytes 7340036 | tf_op jit(solution)/shard_map/dot_general | solution.py:39
  55.6 2.1 collective-permute-start.4
  57.8 12.8 %collective-permute-done.3 = f32[512,256]{0,1:T(8,128)S(1)} collective-permute-done((f32[512,256]{0,1:T(8,128)S(1)}, f32[512,256]{0,1:T(8,128)S(1)}, u32[]{:S(2)}, u32[]{:S(2)}) %collective-permute-start.3) | collective-permute-done | bytes 524320 | tf_op jit(solution)/shard_map/ppermute | solution.py:16
  72.1 10.0 %collective-permute-done.4 = f32[512,256]{0,1:T(8,128)S(1)} collective-permute-done((f32[512,256]{0,1:T(8,128)S(1)}, f32[512,256]{0,1:T(8,128)S(1)}, u32[]{:S(2)}, u32[]{:S(2)}) %collective-permute-start.4) | collective-permute-done | bytes 524320 | tf_op jit(solution)/shard_map/ppermute | solution.py:21
  82.1 9.2 %collective-permute-done.5 = f32[512,256]{0,1:T(8,128)S(1)} collective-permute-done((f32[512,256]{0,1:T(8,128)S(1)}, f32[512,256]{0,1:T(8,128)S(1)}, u32[]{:S(2)}, u32[]{:S(2)}) %collective-permute-start.5) | collective-permute-done | bytes 524320 | tf_op jit(solution)/shard_map/ppermute | solution.py:16
  91.4 3.7 fusion.21
  95.1 3.3 fusion.11
  98.5 35.5 %reduce-scatter.2.cloned.1.call-done = f32[512,256]{1,0:T(8,128)} async-done(((f32[2048,256]{1,0:T(8,128)}), f32[512,256]{1,0:T(8,128)}) %reduce-scatter.2.cloned.1.call-update) | async-done | bytes 524304 | tf_op jit(solution)/shard_map/reduce_scatter | solution.py:105
  135.2 1.5 collective-permute-start.6
  136.9 6.4 %collective-permute-done.6 = f32[2,128,256]{1,2,0:T(8,128)S(1)} collective-permute-done((f32[2,128,256]{1,2,0:T(8,128)S(1)}, f32[2,128,256]{1,2,0:T(8,128)S(1)}, u32[]{:S(2)}, u32[]{:S(2)}) %collective-permute-start.6) | collective-permute-done | bytes 262176 | tf_op jit(solution)/shard_map/ppermute | solution.py:35
  144.8 14.2 %all-gather = f32[1,512,256]{1,2,0:T(8,128)S(1)} all-gather(f32[1,128,256]{1,2,0:T(8,128)S(1)} %add_add_fusion), channel_id=2, replica_groups=mesh['front'=8,'tile'=4] {'tile'}, dimensions={1}, use_global_device_ids=true | all-gather | bytes 655360 | tf_op jit(solution)/shard_map/all_gather | solution.py:61
  159.0 1.9 collective-permute-done.8
  161.1 1.6 collective-permute-start.9
  162.6 23.8 %collective-permute-done.9 = f32[2,512,256]{1,2,0:T(8,128)} collective-permute-done((f32[2,512,256]{1,2,0:T(8,128)S(1)}, f32[2,512,256]{1,2,0:T(8,128)}, u32[]{:S(2)}, u32[]{:S(2)}) %collective-permute-start.9) | collective-permute-done | bytes 1048608 | tf_op jit(solution)/shard_map/ppermute | solution.py:35
  186.5 2.7 maximum_select_fusion
  189.2 1.9 copy.32
  191.0 5.0 %convolution_bitcast_fusion = f32[128,256]{0,1:T(8,128)S(1)} fusion(f32[2048,256]{1,0:T(8,128)} %bitcast.69, f32[1,128,2048]{2,1,0:T(8,128)S(1)} %copy-done), kind=kOutput, calls=%fused_computation.25 | convolution fusion | flops 805306368 | bytes 3276800 | tf_op jit(solution)/shard_map/dot_general | solution.py:39
  196.0 11.5 %all_gather.10 = f32[512,256]{0,1:T(8,128)S(1)} all-gather(f32[128,256]{0,1:T(8,128)S(1)} %convolution_bitcast_fusion), channel_id=1, replica_groups=mesh['front'=8,'tile'=4] {'tile'}, dimensions={0}, use_global_device_ids=true | all-gather | bytes 655360 | tf_op jit(solution)/shard_map/all_gather | solution.py:61
  207.6 1.9 collective-permute-done.10
  211.1 23.7 %collective-permute-done.11 = f32[2,512,256]{1,2,0:T(8,128)S(1)} collective-permute-done((f32[2,512,256]{1,2,0:T(8,128)S(1)}, f32[2,512,256]{1,2,0:T(8,128)S(1)}, u32[]{:S(2)}, u32[]{:S(2)}) %collective-permute-start.11) | collective-permute-done | bytes 1048608 | tf_op jit(solution)/shard_map/ppermute | solution.py:35
  235.2 1.9 copy.33
  237.0 5.0 %fusion.33 = f32[256,128]{1,0:T(8,128)S(1)} fusion(f32[2048,256]{1,0:T(8,128)} %bitcast.70, f32[1,128,2048]{2,1,0:T(8,128)S(1)} %copy-done.7), kind=kOutput, calls=%fused_computation.29 | convolution fusion | flops 805306368 | bytes 3276800 | tf_op jit(solution)/shard_map/dot_general | solution.py:39
  242.0 12.5 %all_gather.11 = f32[512,256]{0,1:T(8,128)S(1)} all-gather(f32[128,256]{0,1:T(8,128)S(1)} %bitcast.76), channel_id=1, replica_groups=mesh['front'=8,'tile'=4] {'tile'}, dimensions={0}, use_global_device_ids=true | all-gather | bytes 655360 | tf_op jit(solution)/shard_map/all_gather | solution.py:61
  254.6 1.9 collective-permute-done.12
  256.6 1.6 collective-permute-start.13
  258.2 23.7 %collective-permute-done.13 = f32[2,512,256]{1,2,0:T(8,128)S(1)} collective-permute-done((f32[2,512,256]{1,2,0:T(8,128)S(1)}, f32[2,512,256]{1,2,0:T(8,128)S(1)}, u32[]{:S(2)}, u32[]{:S(2)}) %collective-permute-start.13) | collective-permute-done | bytes 1048608 | tf_op jit(solution)/shard_map/ppermute | solution.py:35
  282.2 1.9 copy.34
  284.1 4.0 %fusion.9 = f32[512,256]{1,0:T(8,128)S(1)} fusion(f32[2048,256]{1,0:T(8,128)} %bitcast.75, s32[512]{0:T(512)S(1)} %bitcast.82, pred[512]{0:T(512)(128)(4,1)S(1)} %add_compare_fusion), kind=kOutput, calls=%fused_computation.11 | convolution fusion | flops 3223322624 | bytes 2624000 | tf_op jit(solution)/shard_map/dot_general | solution.py:39
  288.7 2.3 collective-permute-start.15
  291.0 12.8 %collective-permute-done.14 = f32[512,256]{1,0:T(8,128)S(1)} collective-permute-done((f32[512,256]{1,0:T(8,128)S(1)}, f32[512,256]{1,0:T(8,128)S(1)}, u32[]{:S(2)}, u32[]{:S(2)}) %collective-permute-start.14) | collective-permute-done | bytes 524320 | tf_op jit(solution)/shard_map/ppermute | solution.py:16
  304.1 1.6 broadcast.99.clone.2
  306.8 7.5 %collective-permute-done.15 = f32[512,256]{1,0:T(8,128)S(1)} collective-permute-done((f32[512,256]{1,0:T(8,128)S(1)}, f32[512,256]{1,0:T(8,128)S(1)}, u32[]{:S(2)}, u32[]{:S(2)}) %collective-permute-start.15) | collective-permute-done | bytes 524320 | tf_op jit(solution)/shard_map/ppermute | solution.py:21
  316.2 8.4 %collective-permute-done.16 = f32[512,256]{1,0:T(8,128)S(1)} collective-permute-done((f32[512,256]{1,0:T(8,128)S(1)}, f32[512,256]{1,0:T(8,128)S(1)}, u32[]{:S(2)}, u32[]{:S(2)}) %collective-permute-start.16) | collective-permute-done | bytes 524320 | tf_op jit(solution)/shard_map/ppermute | solution.py:16
  325.9 6.0 %constant_dynamic-update-slice_fusion.3 = (f32[2048,256]{0,1:T(8,128)S(1)}, f32[512,256]{0,1:T(8,128)S(1)}) fusion(f32[2048,256]{0,1:T(8,128)S(1)} %broadcast.99, s32[]{:T(128)S(6)} %select_n.182, f32[512,256]{0,1:T(8,128)S(1)} %copy-done.6, f32[2048,256]{0,1:T(8,128)} %constant_dynamic-update-slice_fusion.4, f32[1,512,2048]{2,1,0:T(8,128)} %param.13), kind=kOutput, calls=%fused_computation.41 | convolution fusion | flops 3221356544 | bytes 7864324 | tf_op jit(solution)/shard_map/dot_general | solution.py:39
  332.0 2.9 collective-permute-start.18
  334.9 12.8 %collective-permute-done.17 = f32[512,256]{0,1:T(8,128)S(1)} collective-permute-done((f32[512,256]{0,1:T(8,128)S(1)}, f32[512,256]{0,1:T(8,128)S(1)}, u32[]{:S(2)}, u32[]{:S(2)}) %collective-permute-start.17) | collective-permute-done | bytes 524320 | tf_op jit(solution)/shard_map/ppermute | solution.py:16
  348.6 9.7 %collective-permute-done.18 = f32[512,256]{0,1:T(8,128)} collective-permute-done((f32[512,256]{0,1:T(8,128)S(1)}, f32[512,256]{0,1:T(8,128)}, u32[]{:S(2)}, u32[]{:S(2)}) %collective-permute-start.18) | collective-permute-done | bytes 524320 | tf_op jit(solution)/shard_map/ppermute | solution.py:21
  359.4 8.3 %collective-permute-done.19 = f32[512,256]{0,1:T(8,128)} collective-permute-done((f32[512,256]{0,1:T(8,128)S(1)}, f32[512,256]{0,1:T(8,128)}, u32[]{:S(2)}, u32[]{:S(2)}) %collective-permute-start.19) | collective-permute-done | bytes 524320 | tf_op jit(solution)/shard_map/ppermute | solution.py:16
  368.8 6.8 %fusion.27 = f32[1,512,256]{1,2,0:T(8,128)} fusion(f32[2048,256]{0,1:T(8,128)S(1)} %constant_dynamic-update-slice_fusion, f32[1,512,2048]{2,1,0:T(8,128)} %param.14), kind=kOutput, calls=%fused_computation.23 | convolution fusion | flops 3221225472 | bytes 6815744 | tf_op jit(solution)/shard_map/dot_general | solution.py:39
  375.6 2.0 copy.39
  (70 shorter events, 21.9 us)
Async XLA Ops:
  7.2 183.8 %copy-start = (f32[1,128,2048]{2,1,0:T(8,128)S(1)}, f32[1,128,2048]{2,1,0:T(8,128)}, u32[]{:S(2)}) copy-start(f32[1,128,2048]{2,1,0:T(8,128)} %param.16) | copy-start | bytes 3145732
  7.2 126.8 %reduce-scatter.2.cloned.1.call-start = ((), (), s32[]{:S(2)}) async-start(), calls=%async_computation.1 | async-start | bytes 2621440 | tf_op jit(solution)/shard_map/reduce_scatter | solution.py:105
  7.2 17.0 %collective-permute-start = (f32[512,256]{1,0:T(8,128)}, f32[512,256]{1,0:T(8,128)}, u32[]{:S(2)}, u32[]{:S(2)}) collective-permute-start(f32[512,256]{1,0:T(8,128)} %bitcast.79), channel_id=1, source_target_pairs={{0,1},{1,2},{2,3},{3,0},{4,5},{5,6},{6,7},{7,4},{8,9},{9,10},{10,1... | collective-permute-start | bytes 1572872 | tf_op jit(solution)/shard_map/ppermute | solution.py:16
  10.2 25.8 %collective-permute-start.1 = (f32[512,256]{1,0:T(8,128)}, f32[512,256]{1,0:T(8,128)}, u32[]{:S(2)}, u32[]{:S(2)}) collective-permute-start(f32[512,256]{1,0:T(8,128)} %bitcast.80), channel_id=1, source_target_pairs={{0,3},{1,0},{2,1},{3,2},{4,7},{5,4},{6,5},{7,6},{8,11},{9,8},{10,9... | collective-permute-start | bytes 1572872 | tf_op jit(solution)/shard_map/ppermute | solution.py:21
  24.2 21.6 %collective-permute-start.2 = (f32[512,256]{1,0:T(8,128)}, f32[512,256]{1,0:T(8,128)}, u32[]{:S(2)}, u32[]{:S(2)}) collective-permute-start(f32[512,256]{1,0:T(8,128)} %collective-permute-done), channel_id=1, source_target_pairs={{0,1},{1,2},{2,3},{3,0},{4,5},{5,6},{6,7},{7,4},{8,9},{9,10},{10,1... | collective-permute-start | bytes 1572872 | tf_op jit(solution)/shard_map/ppermute | solution.py:16
  27.4 1.0 copy-start.4
  49.2 42.1 %copy-start.3 = (f32[1,512,2048]{2,1,0:T(8,128)S(1)}, f32[1,512,2048]{2,1,0:T(8,128)}, u32[]{:S(2)}) copy-start(f32[1,512,2048]{2,1,0:T(8,128)} %param.12) | copy-start | bytes 12582916
  54.8 40.3 %copy-start.5 = (f32[512,256]{0,1:T(8,128)}, f32[512,256]{0,1:T(8,128)S(1)}, u32[]{:S(2)}) copy-start(f32[512,256]{0,1:T(8,128)S(1)} %get-tuple-element.11) | copy-start | bytes 1572868
  54.8 15.8 %collective-permute-start.3 = (f32[512,256]{0,1:T(8,128)S(1)}, f32[512,256]{0,1:T(8,128)S(1)}, u32[]{:S(2)}, u32[]{:S(2)}) collective-permute-start(f32[512,256]{0,1:T(8,128)S(1)} %get-tuple-element.11), channel_id=1, source_target_pairs={{0,1},{1,2},{2,3},{3,0},{4,5},{5,6},{6,7},{7,4},{8,9},{9,10},{10,1... | collective-permute-start | bytes 1572872 | tf_op jit(solution)/shard_map/ppermute | solution.py:16
  55.6 26.5 %collective-permute-start.4 = (f32[512,256]{0,1:T(8,128)S(1)}, f32[512,256]{0,1:T(8,128)S(1)}, u32[]{:S(2)}, u32[]{:S(2)}) collective-permute-start(f32[512,256]{0,1:T(8,128)S(1)} %get-tuple-element.11), channel_id=1, source_target_pairs={{0,3},{1,0},{2,1},{3,2},{4,7},{5,4},{6,5},{7,6},{8,11},{9,8},{10,9... | collective-permute-start | bytes 1572872 | tf_op jit(solution)/shard_map/ppermute | solution.py:21
  70.6 20.7 %collective-permute-start.5 = (f32[512,256]{0,1:T(8,128)S(1)}, f32[512,256]{0,1:T(8,128)S(1)}, u32[]{:S(2)}, u32[]{:S(2)}) collective-permute-start(f32[512,256]{0,1:T(8,128)S(1)} %collective-permute-done.3), channel_id=1, source_target_pairs={{0,1},{1,2},{2,3},{3,0},{4,5},{5,6},{6,7},{7,4},{8,9},{9,10},{10,1... | collective-permute-start | bytes 1572872 | tf_op jit(solution)/shard_map/ppermute | solution.py:16
  98.4 45.0 %copy-start.8 = (f32[1,128,256]{2,1,0:T(8,128)S(1)}, f32[1,128,256]{2,1,0:T(8,128)}, u32[]{:S(2)}) copy-start(f32[1,128,256]{2,1,0:T(8,128)} %param.15) | copy-start | bytes 393220
  135.2 8.1 %collective-permute-start.6 = (f32[2,128,256]{1,2,0:T(8,128)S(1)}, f32[2,128,256]{1,2,0:T(8,128)S(1)}, u32[]{:S(2)}, u32[]{:S(2)}) collective-permute-start(f32[2,128,256]{1,2,0:T(8,128)S(1)} %copy.42), channel_id=1, source_target_pairs={{0,8},{8,0},{4,12},{12,4},{16,24},{24,16},{20,28},{28,20},{1,9},{9... | collective-permute-start | bytes 786440 | tf_op jit(solution)/shard_map/ppermute | solution.py:35
  143.4 1.4 collective-permute-start.7
  159.0 1.9 collective-permute-start.8
  161.1 1.6 copy-start.2
  161.1 25.4 %collective-permute-start.9 = (f32[2,512,256]{1,2,0:T(8,128)S(1)}, f32[2,512,256]{1,2,0:T(8,128)}, u32[]{:S(2)}, u32[]{:S(2)}) collective-permute-start(f32[2,512,256]{1,2,0:T(8,128)S(1)} %maximum_select_fusion.3), channel_id=1, source_target_pairs={{0,8},{8,0},{4,12},{12,4},{16,24},{24,16},{20,28},{28,20},{1,9},{9... | collective-permute-start | bytes 3145736 | tf_op jit(solution)/shard_map/ppermute | solution.py:35
  207.6 1.9 collective-permute-start.10
  209.6 25.3 %collective-permute-start.11 = (f32[2,512,256]{1,2,0:T(8,128)S(1)}, f32[2,512,256]{1,2,0:T(8,128)S(1)}, u32[]{:S(2)}, u32[]{:S(2)}) collective-permute-start(f32[2,512,256]{1,2,0:T(8,128)S(1)} %maximum_select_fusion.4), channel_id=1, source_target_pairs={{0,8},{8,0},{4,12},{12,4},{16,24},{24,16},{20,28},{28,20},{1,9},{9... | collective-permute-start | bytes 3145736 | tf_op jit(solution)/shard_map/ppermute | solution.py:35
  235.2 1.9 copy-start.7
  254.6 1.9 collective-permute-start.12
  256.6 25.3 %collective-permute-start.13 = (f32[2,512,256]{1,2,0:T(8,128)S(1)}, f32[2,512,256]{1,2,0:T(8,128)S(1)}, u32[]{:S(2)}, u32[]{:S(2)}) collective-permute-start(f32[2,512,256]{1,2,0:T(8,128)S(1)} %maximum_select_fusion.5), channel_id=1, source_target_pairs={{0,8},{8,0},{4,12},{12,4},{16,24},{24,16},{20,28},{28,20},{1,9},{9... | collective-permute-start | bytes 3145736 | tf_op jit(solution)/shard_map/ppermute | solution.py:35
  288.1 15.8 %collective-permute-start.14 = (f32[512,256]{1,0:T(8,128)S(1)}, f32[512,256]{1,0:T(8,128)S(1)}, u32[]{:S(2)}, u32[]{:S(2)}) collective-permute-start(f32[512,256]{1,0:T(8,128)S(1)} %fusion.9), channel_id=1, source_target_pairs={{0,1},{1,2},{2,3},{3,0},{4,5},{5,6},{6,7},{7,4},{8,9},{9,10},{10,1... | collective-permute-start | bytes 1572872 | tf_op jit(solution)/shard_map/ppermute | solution.py:16
  288.7 25.5 %collective-permute-start.15 = (f32[512,256]{1,0:T(8,128)S(1)}, f32[512,256]{1,0:T(8,128)S(1)}, u32[]{:S(2)}, u32[]{:S(2)}) collective-permute-start(f32[512,256]{1,0:T(8,128)S(1)} %fusion.9), channel_id=1, source_target_pairs={{0,3},{1,0},{2,1},{3,2},{4,7},{5,4},{6,5},{7,6},{8,11},{9,8},{10,9... | collective-permute-start | bytes 1572872 | tf_op jit(solution)/shard_map/ppermute | solution.py:21
  303.9 20.7 %collective-permute-start.16 = (f32[512,256]{1,0:T(8,128)S(1)}, f32[512,256]{1,0:T(8,128)S(1)}, u32[]{:S(2)}, u32[]{:S(2)}) collective-permute-start(f32[512,256]{1,0:T(8,128)S(1)} %collective-permute-done.14), channel_id=1, source_target_pairs={{0,1},{1,2},{2,3},{3,0},{4,5},{5,6},{6,7},{7,4},{8,9},{9,10},{10,1... | collective-permute-start | bytes 1572872 | tf_op jit(solution)/shard_map/ppermute | solution.py:16
  316.2 9.7 %copy-start.6 = (f32[512,256]{0,1:T(8,128)S(1)}, f32[512,256]{0,1:T(8,128)}, u32[]{:S(2)}) copy-start(f32[512,256]{0,1:T(8,128)} %copy-done.5) | copy-start | bytes 1572868
  332.0 15.8 %collective-permute-start.17 = (f32[512,256]{0,1:T(8,128)S(1)}, f32[512,256]{0,1:T(8,128)S(1)}, u32[]{:S(2)}, u32[]{:S(2)}) collective-permute-start(f32[512,256]{0,1:T(8,128)S(1)} %get-tuple-element.13), channel_id=1, source_target_pairs={{0,1},{1,2},{2,3},{3,0},{4,5},{5,6},{6,7},{7,4},{8,9},{9,10},{10,1... | collective-permute-start | bytes 1572872 | tf_op jit(solution)/shard_map/ppermute | solution.py:16
  332.0 26.3 %collective-permute-start.18 = (f32[512,256]{0,1:T(8,128)S(1)}, f32[512,256]{0,1:T(8,128)}, u32[]{:S(2)}, u32[]{:S(2)}) collective-permute-start(f32[512,256]{0,1:T(8,128)S(1)} %get-tuple-element.13), channel_id=1, source_target_pairs={{0,3},{1,0},{2,1},{3,2},{4,7},{5,4},{6,5},{7,6},{8,11},{9,8},{10,9... | collective-permute-start | bytes 1572872 | tf_op jit(solution)/shard_map/ppermute | solution.py:21
  347.8 19.9 %collective-permute-start.19 = (f32[512,256]{0,1:T(8,128)S(1)}, f32[512,256]{0,1:T(8,128)}, u32[]{:S(2)}, u32[]{:S(2)}) collective-permute-start(f32[512,256]{0,1:T(8,128)S(1)} %collective-permute-done.17), channel_id=1, source_target_pairs={{0,1},{1,2},{2,3},{3,0},{4,5},{5,6},{6,7},{7,4},{8,9},{9,10},{10,1... | collective-permute-start | bytes 1572872 | tf_op jit(solution)/shard_map/ppermute | solution.py:16
  368.8 8.8 %copy-start.1 = (f32[1,128,2048]{2,1,0:T(8,128)S(1)}, f32[1,128,2048]{2,1,0:T(8,128)}, u32[]{:S(2)}) copy-start(f32[1,128,2048]{2,1,0:T(8,128)} %param.16) | copy-start | bytes 3145732
Sparse Core Ops, SparseCore 0:
  98.6 35.3 reduce-scatter.1
